TPU v7x, 32 devices: a whole 2x2x4 slice. The times are simulated.
32 devices in a mesh: bulk: 4 (over x, core), grid: 8 (over z, y).
Axes of the slice: x: 2, y: 2, z: 4, core: 2. Of those that a mesh axis runs over, the one named last changes fastest.
Arguments:
- offsets: float32 [8, 3, 4, 24, 128], P('grid', None, 'bulk'), may hold values from -0.75 to 0.75
- flow: float32 [8, 5, 4, 24, 128], P('grid', None, 'bulk'), may hold values from -6 to 6
- control_points: float32 [3, 16384], P(None, ('bulk', 'grid')), may hold values from -7 to 13
- rbf_weights: float32 [3, 16384], P(None, ('bulk', 'grid')), may hold values from -2 to 2
- peer_offset: int32 [8, 720, 1], P('grid', 'bulk'), may hold values from 0 to 6; in each aligned block of 180 rows (0 to 179, 180 to 359, ..., all dimensions but the last counted through in order) at most 28 rows name the same one
- donor_block: int32 [8, 720], P('grid', 'bulk'), may hold values from 0 to 23
- receptor_block: int32 [8, 720], P('grid', 'bulk'), may hold values from 0 to 23
Outputs:
- moved: float32 [8, 3, 4, 24, 128], P('grid', None, 'bulk')
- metric: float32 [8, 4, 24, 128], P('grid', 'bulk')
- fringe: float32 [8, 5, 4, 24, 128], P('grid', None, 'bulk')
Inputs may be any that keep to these rules, and one draw needn't show every extreme that they name: `peer_offset`: in the 180 rows of one device no value appears more than 28 times.
All inputs are finite; a program needn't handle non-finite values.
Results may differ from a plain program's by a relative error of at most 0.0003.
Values sent between devices are 32-bit elements; how exact they have to be, the bound alone decides.
A program may use at most 64 MiB of HBM per device.

v0:
```python
import math
import jax
import jax.numpy as jnp
from jax import lax
from jax.sharding import PartitionSpec as P

CAP = 28
HIGHEST = lax.Precision.HIGHEST
SUPPORT = 1.25
point_block = 2048


def padded_2(cells, sides, width):
    for axis, dim in sides:
        count = lax.axis_size(axis)
        head = lax.slice_in_dim(cells, 0, width, axis=dim)
        tail = lax.slice_in_dim(cells, cells.shape[dim] - width, cells.shape[dim], axis=dim)
        cells = jnp.concatenate(
            [
                lax.ppermute(tail, axis, [(i, (i + 1) % count) for i in range(count)]),
                cells,
                lax.ppermute(head, axis, [((i + 1) % count, i) for i in range(count)]),
            ],
            axis=dim,
        )
    return cells


def lattice(grid_ids, plane_ids, planes_total, radial, lines):
    theta = 2.0 * math.pi * plane_ids.astype(jnp.float32) / planes_total
    radius = 1.0 + 0.25 * jnp.arange(radial, dtype=jnp.float32)
    height = 0.1 * jnp.arange(lines, dtype=jnp.float32)
    centre = 0.5 * grid_ids.astype(jnp.float32)
    xcoord = (
        centre[:, None, None, None]
        + radius[None, None, :, None] * jnp.cos(theta)[None, :, None, None]
        + 0.0 * height[None, None, None, :]
    )
    ycoord = (radius[None, :, None] * jnp.sin(theta)[:, None, None] + 0.0 * height[None, None, :])[
        None
    ] + 0.0 * centre[:, None, None, None]
    zcoord = jnp.zeros_like(xcoord) + height[None, None, None, :]
    return jnp.stack([xcoord, ycoord, zcoord], axis=1)


def kernel_sum(nodes, points, weights):
    squared = (nodes[0][:, None] - points[0][None, :]) ** 2
    squared = squared + (nodes[1][:, None] - points[1][None, :]) ** 2
    squared = squared + (nodes[2][:, None] - points[2][None, :]) ** 2
    scaled = jnp.sqrt(squared) / SUPPORT
    inside = jnp.maximum(1.0 - scaled, 0.0)
    basis = inside**4 * (4.0 * scaled + 1.0)
    return jnp.einsum("ck,nk->cn", weights, basis, precision=HIGHEST)


def deck_terms(carry, nodes, points, weights):
    breadth = points.shape[1]
    tile_width = math.gcd(breadth, point_block)
    turns = breadth // tile_width

    def one_tile(tile_number, running):
        tile_points = lax.dynamic_slice_in_dim(points, tile_number * tile_width, tile_width, 1)
        tile_weights = lax.dynamic_slice_in_dim(weights, tile_number * tile_width, tile_width, 1)
        return running + kernel_sum(nodes, tile_points, tile_weights)

    return lax.fori_loop(0, turns, one_tile, carry)


def along_axis(field, axis):
    total = field.shape[axis]
    ahead = lax.slice_in_dim(field, 2, total, axis=axis)
    behind = lax.slice_in_dim(field, 0, total - 2, axis=axis)
    first = lax.slice_in_dim(field, 1, 2, axis=axis) - lax.slice_in_dim(field, 0, 1, axis=axis)
    last = lax.slice_in_dim(field, total - 1, total, axis=axis) - lax.slice_in_dim(
        field, total - 2, total - 1, axis=axis
    )
    return jnp.concatenate([first, (ahead - behind) * 0.5, last], axis=axis)


def jacobian(slope_plane, slope_radial, slope_height):
    cross_x = slope_radial[:, 1] * slope_height[:, 2] - slope_radial[:, 2] * slope_height[:, 1]
    cross_y = slope_radial[:, 2] * slope_height[:, 0] - slope_radial[:, 0] * slope_height[:, 2]
    cross_z = slope_radial[:, 0] * slope_height[:, 1] - slope_radial[:, 1] * slope_height[:, 0]
    return slope_plane[:, 0] * cross_x + slope_plane[:, 1] * cross_y + slope_plane[:, 2] * cross_z


def blend(receptor_xyz, donor_xyz, donor_values):
    squared = (receptor_xyz[:, 0, :, None] - donor_xyz[:, 0, None, :]) ** 2
    squared = squared + (receptor_xyz[:, 1, :, None] - donor_xyz[:, 1, None, :]) ** 2
    squared = squared + (receptor_xyz[:, 2, :, None] - donor_xyz[:, 2, None, :]) ** 2
    weight = 1.0 / (0.25 + squared)
    totals = jnp.sum(weight, axis=2)
    weighted = jnp.einsum("nad,nvd->nva", weight, donor_values, precision=HIGHEST)
    return weighted / totals[:, None, :]


def blend_group(items):
    receptor_xyz, donor = items
    return blend(receptor_xyz, donor[:, :3], donor[:, 3:])


def local(offsets, flow, control_points, rbf_weights, peer_offset, donor_block, receptor_block):
    planes = offsets.shape[2]
    radial = offsets.shape[3]
    lines = offsets.shape[4]
    blocks = planes * radial
    grids = lax.axis_size("grid")
    grid_here = lax.axis_index("grid")
    plane_ids = lax.axis_index("bulk") * planes + jnp.arange(planes, dtype=jnp.int32)
    base = (
        lattice(grid_here[None], plane_ids, planes * lax.axis_size("bulk"), radial, lines) + offsets
    )
    nodes = base[0].reshape(3, -1)
    empty = jnp.zeros(nodes.shape, jnp.float32)
    all_points, all_weights = (
        lax.all_gather(control_points, ("bulk", "grid"), axis=1, tiled=True),
        lax.all_gather(rbf_weights, ("bulk", "grid"), axis=1, tiled=True),
    )
    shifts = deck_terms(empty, nodes, all_points, all_weights)
    moved = base + shifts.reshape(base.shape)
    padded = padded_2(moved, (("bulk", 2),), 1)
    slope_plane = (padded[:, :, 2:] - padded[:, :, :-2]) * 0.5
    slope_radial = along_axis(moved, 3)
    slope_height = along_axis(moved, 4)
    metric = jacobian(slope_plane, slope_radial, slope_height)
    values = metric[:, None] * flow
    payload = jnp.concatenate([moved, values], axis=1)[0].reshape(-1, blocks, lines)
    coords = moved[0].reshape(3, blocks, lines)
    block_iota = jnp.arange(blocks, dtype=jnp.int32)
    pick_donor = (donor_block[0][:, None] == block_iota[None, :]).astype(jnp.float32)
    chosen = jnp.einsum("sb,cbk->sck", pick_donor, payload, precision=HIGHEST)
    receiver = (grid_here + 1 + peer_offset[0, :, 0]) % grids
    receiver_hot = (receiver[:, None] == jnp.arange(grids, dtype=jnp.int32)[None, :]).astype(
        jnp.int32
    )
    before = jnp.cumsum(receiver_hot, axis=0) - receiver_hot
    position = jnp.sum(before * receiver_hot, axis=1)
    capacity = CAP
    target = receiver * capacity + position
    place = (jnp.arange(grids * capacity, dtype=jnp.int32)[:, None] == target[None, :]).astype(
        jnp.float32
    )
    label = (receptor_block[0] + 1).astype(jnp.float32)
    label_sent = jnp.einsum("ts,s->t", place, label, precision=HIGHEST).reshape(grids, capacity)
    sent = jnp.einsum("ts,sck->tck", place, chosen, precision=HIGHEST).reshape(
        grids, capacity, -1, lines
    )
    arrived, arrived_label = (
        lax.all_to_all(sent, "grid", split_axis=0, concat_axis=0, tiled=True),
        lax.all_to_all(label_sent, "grid", split_axis=0, concat_axis=0, tiled=True),
    )
    pick_receptor = (
        arrived_label.reshape(-1)[:, None] == (block_iota + 1).astype(jnp.float32)[None, :]
    ).astype(jnp.float32)
    receptor_xyz = jnp.einsum("tb,cbk->tck", pick_receptor, coords, precision=HIGHEST).reshape(
        grids, capacity, 3, lines
    )
    interpolated = lax.map(blend_group, (receptor_xyz, arrived)).reshape(
        grids * capacity, -1, lines
    )
    fringe = jnp.einsum("tb,tvk->vbk", pick_receptor, interpolated, precision=HIGHEST)
    return (moved, metric, fringe.reshape(1, -1, planes, radial, lines))


def solution(mesh):
    in_specs = (
        P("grid", None, "bulk", None, None),
        P("grid", None, "bulk", None, None),
        P(None, ("bulk", "grid")),
        P(None, ("bulk", "grid")),
        P("grid", "bulk", None),
        P("grid", "bulk"),
        P("grid", "bulk"),
    )
    out_specs = (
        P("grid", None, "bulk", None, None),
        P("grid", "bulk", None, None),
        P("grid", None, "bulk", None, None),
    )
    return jax.shard_map(local, mesh=mesh, in_specs=in_specs, out_specs=out_specs, check_vma=False)
```

profile of v0, /device:TPU:0, one launch (start us, length us, event | category | flops | bytes accessed | tf_op | source)
XLA Modules:
  0.0 534.4 jit_solution(6957581617032053949)
XLA Ops:
  1.7 71.5 %all_gather.7 = f32[3,16384]{1,0:T(4,128)S(1)} all-gather(f32[3,512]{1,0:T(4,128)} %param.13), channel_id=1, replica_groups=mesh['bulk'=4,'grid'=8] {'bulk','grid'}, dimensions={1}, use_global_device_ids=true | all-gather | bytes 202752 | tf_op jit(solution)/shard_map/all_gather | solution.py:116
  73.2 65.0 %all_gather.6 = f32[3,16384]{1,0:T(4,128)S(1)} all-gather(f32[3,512]{1,0:T(4,128)} %param.14), channel_id=1, replica_groups=mesh['bulk'=4,'grid'=8] {'bulk','grid'}, dimensions={1}, use_global_device_ids=true | all-gather | bytes 202752 | tf_op jit(solution)/shard_map/all_gather | solution.py:117
  138.2 300.2 %while.27 = (s32[]{:T(128)}, f32[3,3072]{1,0:T(4,128)S(1)}, f32[3,16384]{1,0:T(4,128)S(1)}, f32[3,3072]{1,0:T(4,128)S(1)}, f32[3,16384]{1,0:T(4,128)S(1)}, /*ind...) while((s32[]{:T(128)}, f32[3,3072]{1,0:T(4,128)S(1)}, ...), condition=%wide.region_1.0_spmd.clone, body=%wide.region_0.0_spmd.clone.sunk | while | flops 327174144 | bytes 303317 | solution.py:66
  138.3 37.3 %fusion.98 = f32[3,3072]{1,0:T(4,128)S(1)} fusion(f32[2048]{0:T(1024)S(1)} %bitcast.128, f32[3072]{0:T(1024)S(1)} %bitcast.124, f32[2048]{0:T(1024)S(1)} %bitcast.127, f32[3072]{0:T(1024)S(1)} %bitcast.125, f32[2048]{0:T(1024)S(1)} %bitcast.126, f32[3072]{0:T(1024)S(1)} %bitcast.123, f32[3,3072]{1,0:T(4,128)S(1)} %get-tuple-element.325, ...), kind=kOutput, calls=%fused_computation.44.clone.1 | convolution fusion | flops 327174144 | bytes 180229 | tf_op jit(solution)/shard_map/while/body/eval_jaxpr/ck,nk->cn/dot_general | solution.py:53
  175.8 37.3 %fusion.98 = f32[3,3072]{1,0:T(4,128)S(1)} fusion(f32[2048]{0:T(1024)S(1)} %bitcast.128, f32[3072]{0:T(1024)S(1)} %bitcast.124, f32[2048]{0:T(1024)S(1)} %bitcast.127, f32[3072]{0:T(1024)S(1)} %bitcast.125, f32[2048]{0:T(1024)S(1)} %bitcast.126, f32[3072]{0:T(1024)S(1)} %bitcast.123, f32[3,3072]{1,0:T(4,128)S(1)} %get-tuple-element.325, ...), kind=kOutput, calls=%fused_computation.44.clone.1 | convolution fusion | flops 327174144 | bytes 180229 | tf_op jit(solution)/shard_map/while/body/eval_jaxpr/ck,nk->cn/dot_general | solution.py:53
  213.3 37.3 %fusion.98 = f32[3,3072]{1,0:T(4,128)S(1)} fusion(f32[2048]{0:T(1024)S(1)} %bitcast.128, f32[3072]{0:T(1024)S(1)} %bitcast.124, f32[2048]{0:T(1024)S(1)} %bitcast.127, f32[3072]{0:T(1024)S(1)} %bitcast.125, f32[2048]{0:T(1024)S(1)} %bitcast.126, f32[3072]{0:T(1024)S(1)} %bitcast.123, f32[3,3072]{1,0:T(4,128)S(1)} %get-tuple-element.325, ...), kind=kOutput, calls=%fused_computation.44.clone.1 | convolution fusion | flops 327174144 | bytes 180229 | tf_op jit(solution)/shard_map/while/body/eval_jaxpr/ck,nk->cn/dot_general | solution.py:53
  250.8 37.3 %fusion.98 = f32[3,3072]{1,0:T(4,128)S(1)} fusion(f32[2048]{0:T(1024)S(1)} %bitcast.128, f32[3072]{0:T(1024)S(1)} %bitcast.124, f32[2048]{0:T(1024)S(1)} %bitcast.127, f32[3072]{0:T(1024)S(1)} %bitcast.125, f32[2048]{0:T(1024)S(1)} %bitcast.126, f32[3072]{0:T(1024)S(1)} %bitcast.123, f32[3,3072]{1,0:T(4,128)S(1)} %get-tuple-element.325, ...), kind=kOutput, calls=%fused_computation.44.clone.1 | convolution fusion | flops 327174144 | bytes 180229 | tf_op jit(solution)/shard_map/while/body/eval_jaxpr/ck,nk->cn/dot_general | solution.py:53
  288.3 37.3 %fusion.98 = f32[3,3072]{1,0:T(4,128)S(1)} fusion(f32[2048]{0:T(1024)S(1)} %bitcast.128, f32[3072]{0:T(1024)S(1)} %bitcast.124, f32[2048]{0:T(1024)S(1)} %bitcast.127, f32[3072]{0:T(1024)S(1)} %bitcast.125, f32[2048]{0:T(1024)S(1)} %bitcast.126, f32[3072]{0:T(1024)S(1)} %bitcast.123, f32[3,3072]{1,0:T(4,128)S(1)} %get-tuple-element.325, ...), kind=kOutput, calls=%fused_computation.44.clone.1 | convolution fusion | flops 327174144 | bytes 180229 | tf_op jit(solution)/shard_map/while/body/eval_jaxpr/ck,nk->cn/dot_general | solution.py:53
  325.8 37.3 %fusion.98 = f32[3,3072]{1,0:T(4,128)S(1)} fusion(f32[2048]{0:T(1024)S(1)} %bitcast.128, f32[3072]{0:T(1024)S(1)} %bitcast.124, f32[2048]{0:T(1024)S(1)} %bitcast.127, f32[3072]{0:T(1024)S(1)} %bitcast.125, f32[2048]{0:T(1024)S(1)} %bitcast.126, f32[3072]{0:T(1024)S(1)} %bitcast.123, f32[3,3072]{1,0:T(4,128)S(1)} %get-tuple-element.325, ...), kind=kOutput, calls=%fused_computation.44.clone.1 | convolution fusion | flops 327174144 | bytes 180229 | tf_op jit(solution)/shard_map/while/body/eval_jaxpr/ck,nk->cn/dot_general | solution.py:53
  363.3 37.3 %fusion.98 = f32[3,3072]{1,0:T(4,128)S(1)} fusion(f32[2048]{0:T(1024)S(1)} %bitcast.128, f32[3072]{0:T(1024)S(1)} %bitcast.124, f32[2048]{0:T(1024)S(1)} %bitcast.127, f32[3072]{0:T(1024)S(1)} %bitcast.125, f32[2048]{0:T(1024)S(1)} %bitcast.126, f32[3072]{0:T(1024)S(1)} %bitcast.123, f32[3,3072]{1,0:T(4,128)S(1)} %get-tuple-element.325, ...), kind=kOutput, calls=%fused_computation.44.clone.1 | convolution fusion | flops 327174144 | bytes 180229 | tf_op jit(solution)/shard_map/while/body/eval_jaxpr/ck,nk->cn/dot_general | solution.py:53
  400.8 37.3 %fusion.98 = f32[3,3072]{1,0:T(4,128)S(1)} fusion(f32[2048]{0:T(1024)S(1)} %bitcast.128, f32[3072]{0:T(1024)S(1)} %bitcast.124, f32[2048]{0:T(1024)S(1)} %bitcast.127, f32[3072]{0:T(1024)S(1)} %bitcast.125, f32[2048]{0:T(1024)S(1)} %bitcast.126, f32[3072]{0:T(1024)S(1)} %bitcast.123, f32[3,3072]{1,0:T(4,128)S(1)} %get-tuple-element.325, ...), kind=kOutput, calls=%fused_computation.44.clone.1 | convolution fusion | flops 327174144 | bytes 180229 | tf_op jit(solution)/shard_map/while/body/eval_jaxpr/ck,nk->cn/dot_general | solution.py:53
  442.3 3.5 all-to-all-start.1
  448.9 3.3 all-to-all-done.1
  452.2 3.6 all-to-all-start
  457.5 19.4 %all-to-all-done = f32[8,28,8,128]{3,2,1,0:T(8,128)S(1)} async-done(((f32[8,28,8,128]{3,2,1,0:T(8,128)}), f32[8,28,8,128]{3,2,1,0:T(8,128)S(1)}, u32[]{:S(2)}, u32[]{:S(2)}) %all-to-all-start) | async-done | bytes 917536 | tf_op jit(solution)/shard_map/all_to_all | solution.py:149
  476.9 56.5 %while.26 = (s32[]{:T(128)}, f32[8,28,5,128]{3,2,1,0:T(8,128)S(1)}, f32[8,28,8,128]{3,2,1,0:T(8,128)S(1)}, f32[8,28,3,128]{3,1,2,0:T(8,128)S(1)}, s32[]{:T(128)}) while((s32[]{:T(128)}, f32[8,28,5,128]{3,2,1,0:T(8,128)S(1)}, f32[8,28,8,128]{3,2,1,0:T(8,128)S(1)}, f32[8,28,3,128]{3,1,2,0:T(8,128)S(1)}, s32[]{:T(128)}) %tuple.87), condition=%wide.region_7.8_spmd, body=%wide.region_5.7_spmd.sunk | while | flops 37173248 | bytes 1017937 | solution.py:158
  476.9 2.4 fusion.93
  479.4 4.5 fusion.94
  484.0 2.4 fusion.93
  486.5 4.5 fusion.94
  491.1 2.4 fusion.93
  493.5 4.5 fusion.94
  498.2 2.4 fusion.93
  500.6 4.5 fusion.94
  505.2 2.4 fusion.93
  507.7 4.5 fusion.94
  512.3 2.4 fusion.93
  514.7 4.5 fusion.94
  519.4 2.4 fusion.93
  521.8 4.5 fusion.94
  526.4 2.4 fusion.93
  528.9 4.5 fusion.94
  (115 shorter events, 12.1 us)
Async XLA Ops:
  138.2 300.2 %copy-start.1 = (f32[1,3,1,24,128]{4,3,2,1,0:T(8,128)S(1)}, f32[1,3,1,24,128]{4,3,2,1,0:T(8,128)}, u32[]{:S(2)}) copy-start(f32[1,3,1,24,128]{4,3,2,1,0:T(8,128)} %param.11) | copy-start | bytes 110596
  138.2 302.1 %copy-start.5 = (s32[1,180,1]{1,2,0:T(1,128)S(1)}, s32[1,180,1]{1,2,0:T(1,128)}, u32[]{:S(2)}) copy-start(s32[1,180,1]{1,2,0:T(1,128)} %param.15) | copy-start | bytes 2164
  138.2 303.1 %copy-start.6 = (s32[1,180]{1,0:T(1,128)S(1)}, s32[1,180]{1,0:T(1,128)}, u32[]{:S(2)}) copy-start(s32[1,180]{1,0:T(1,128)} %param.17) | copy-start | bytes 2164
  438.4 7.8 %copy-start.2 = (f32[1,5,1,24,128]{4,3,2,1,0:T(8,128)S(1)}, f32[1,5,1,24,128]{4,3,2,1,0:T(8,128)}, u32[]{:S(2)}) copy-start(f32[1,5,1,24,128]{4,3,2,1,0:T(8,128)} %param.12) | copy-start | bytes 184324
  438.4 7.8 %copy-start.4 = (s32[1,180]{1,0:T(1,128)S(1)}, s32[1,180]{1,0:T(1,128)}, u32[]{:S(2)}) copy-start(s32[1,180]{1,0:T(1,128)} %param.16) | copy-start | bytes 2164
  438.4 18.6 %copy-start = (f32[1,3,1,24,128]{4,3,1,2,0:T(8,128)}, f32[1,3,1,24,128]{4,3,1,2,0:T(8,128)S(1)}, u32[]{:S(2)}) copy-start(f32[1,3,1,24,128]{4,3,1,2,0:T(8,128)S(1)} %bitcast_add_fusion) | copy-start | bytes 110596
  438.4 7.7 %collective-permute-start.1 = (f32[1,3,1,24,128]{4,3,1,2,0:T(8,128)S(1)}, f32[1,3,1,24,128]{4,3,1,2,0:T(8,128)S(1)}, u32[]{:S(2)}, u32[]{:S(2)}) collective-permute-start(f32[1,3,1,24,128]{4,3,1,2,0:T(8,128)S(1)} %bitcast_add_fusion), channel_id=1, source_target_pairs={{0,8},{8,16},{16,24},{24,0},{1,9},{9,17},{17,25},{25,1},{2,10},{10... | collective-permute-start | bytes 110600 | tf_op jit(solution)/shard_map/ppermute | solution.py:20
  438.5 7.6 %collective-permute-start = (f32[1,3,1,24,128]{4,3,1,2,0:T(8,128)S(1)}, f32[1,3,1,24,128]{4,3,1,2,0:T(8,128)S(1)}, u32[]{:S(2)}, u32[]{:S(2)}) collective-permute-start(f32[1,3,1,24,128]{4,3,1,2,0:T(8,128)S(1)} %bitcast_add_fusion), channel_id=1, source_target_pairs={{8,0},{16,8},{24,16},{0,24},{9,1},{17,9},{25,17},{1,25},{10,2},{18... | collective-permute-start | bytes 110600 | tf_op jit(solution)/shard_map/ppermute | solution.py:22
  442.3 9.9 %all-to-all-start.1 = ((f32[8,1,28]{2,1,0:T(1,128)}), f32[8,1,28]{2,1,0:T(1,128)S(1)}, u32[]{:S(2)}, u32[]{:S(2)}) async-start(f32[8,1,28]{2,1,0:T(1,128)} %convolution_bitcast_fusion.1), calls=%async_computation.1 | async-start | bytes 8192 | tf_op jit(solution)/shard_map/all_to_all | solution.py:150
  446.2 1.2 copy-start.3
  452.2 24.7 %all-to-all-start = ((f32[8,28,8,128]{3,2,1,0:T(8,128)}), f32[8,28,8,128]{3,2,1,0:T(8,128)S(1)}, u32[]{:S(2)}, u32[]{:S(2)}) async-start(f32[8,28,8,128]{3,2,1,0:T(8,128)} %bitcast.19), calls=%async_computation | async-start | bytes 1835008 | tf_op jit(solution)/shard_map/all_to_all | solution.py:149
where the time goes:
time: 535 us; the launch traced here: 534 us
  matrix products  339 us (63%)
  blocking collectives  136 us (25%)
  waiting for transfers between devices  22.7 us (4%)
  other arithmetic  22.2 us (4%)
  starting transfers between devices  8.83 us (2%)
    dot_general x8, matrix products, kernel_sum(): return jnp.einsum('ck,nk->cn', weights, basis, precision=HIGHEST)  299 us
    all_gather x1, blocking collectives, local(): lax.all_gather(control_points, ('bulk', 'grid'), axis=1, tiled=True)  71.5 us
    all_gather x1, blocking collectives, local(): lax.all_gather(rbf_weights, ('bulk', 'grid'), axis=1, tiled=True)  65 us
    dot_general x8, matrix products, blend(): jnp.einsum('nad,nvd->nva', weight, donor_values, precision=HIGHEST)  36.2 us
    reduce_sum x8, other arithmetic, blend(): totals = jnp.sum(weight, axis=2)  19.5 us
    all_to_all x1, waiting for transfers between devices, local(): lax.all_to_all(sent, 'grid', split_axis=0, concat_axis=0, tiled=True)  19.4 us
  transfers between devices with their start and end apart: 4, of which 2 were waited for; matrix products, arithmetic and copies ran while one was open for 1% of the time, Pallas kernels for 0%

commit v1 on v0

--- a/solution.py
+++ b/solution.py
@@ -8,6 +8,28 @@
 HIGHEST = lax.Precision.HIGHEST
 SUPPORT = 1.25
 point_block = 2048
+
+
+def joined_along(pieces, dim):
+    shape = list(pieces.shape[1:])
+    shape[dim] *= pieces.shape[0]
+    return jnp.moveaxis(pieces, 0, dim).reshape(shape)
+
+
+def grow_blocks(value, axis):
+    length = lax.axis_size(axis)
+    blocks = value[None]
+    for level in range(length.bit_length() - 1):
+        bit = 1 << level
+        received = lax.ppermute(blocks, axis, [(i, i ^ bit) for i in range(length)])
+        both = jnp.stack([blocks, received])
+        upper = lax.axis_index(axis) >> level & 1
+        blocks = jnp.where(upper == 0, both, both[::-1]).reshape(-1, *value.shape)
+    return blocks
+
+
+def collect(shard, axis, dim):
+    return joined_along(grow_blocks(shard, axis), dim)
 
 
 def padded_2(cells, sides, width):
@@ -114,7 +136,7 @@
     empty = jnp.zeros(nodes.shape, jnp.float32)
     all_points, all_weights = (
         lax.all_gather(control_points, ("bulk", "grid"), axis=1, tiled=True),
-        lax.all_gather(rbf_weights, ("bulk", "grid"), axis=1, tiled=True),
+        collect(rbf_weights, ("bulk", "grid"), 1),
     )
     shifts = deck_terms(empty, nodes, all_points, all_weights)
     moved = base + shifts.reshape(base.shape)

time: 535 us -> 489 us (0.914)
  blocking collectives: 136 us -> 69.3 us
  starting transfers between devices: 8.83 us -> 21.5 us
  waiting for transfers between devices: 22.7 us -> 30.1 us
    all_gather x1 -> x0, blocking collectives: 65 us -> none  [local(): lax.all_gather(rbf_weights, ('bulk', 'grid'), axis=1, tiled=True)]
    ppermute x0 -> x5, starting transfers between devices: none -> 8.86 us  [grow_blocks(): received = lax.ppermute(blocks, axis, [(i, i ^ bit) for i in range(length)])]
    ppermute x0 -> x5, waiting for transfers between devices: none -> 6.44 us  [grow_blocks(): received = lax.ppermute(blocks, axis, [(i, i ^ bit) for i in range(length)])]
  transfers between devices with their start and end apart: 4 -> 9, of which waited for: 2 -> 6; matrix products, arithmetic and copies ran while one was open for 1% -> 62% of each run, Pallas kernels for 0% -> 0%
where the time goes in v1:
time: 489 us
  matrix products  339 us (69%)
  blocking collectives  69.3 us (14%)
  waiting for transfers between devices  30.1 us (6%)
  other arithmetic  22.9 us (5%)
  starting transfers between devices  21.5 us (4%)
    dot_general x8, matrix products, kernel_sum(): return jnp.einsum('ck,nk->cn', weights, basis, precision=HIGHEST)  299 us
    all_gather x1, blocking collectives, local(): lax.all_gather(control_points, ('bulk', 'grid'), axis=1, tiled=True)  69.3 us
    dot_general x8, matrix products, blend(): jnp.einsum('nad,nvd->nva', weight, donor_values, precision=HIGHEST)  36.2 us
    all_to_all x1, waiting for transfers between devices, local(): lax.all_to_all(sent, 'grid', split_axis=0, concat_axis=0, tiled=True)  22.2 us
    reduce_sum x8, other arithmetic, blend(): totals = jnp.sum(weight, axis=2)  19.5 us
  transfers between devices with their start and end apart: 9, of which 6 were waited for; matrix products, arithmetic and copies ran while one was open for 62% of the time, Pallas kernels for 0%

profile of v1, /device:TPU:0, one launch (start us, length us, event | category | flops | bytes accessed | tf_op | source)
XLA Modules:
  0.0 489.0 jit_solution(6064156811481585679)
XLA Ops:
  4.1 7.3 %all-to-all-start.1 = ((f32[8,1,28]{2,1,0:T(1,128)}), f32[8,1,28]{2,1,0:T(1,128)S(1)}, u32[]{:S(2)}, u32[]{:S(2)}) async-start(f32[8,1,28]{2,1,0:T(1,128)} %convolution_bitcast_fusion.1), calls=%async_computation.1 | async-start | bytes 8192 | tf_op jit(solution)/shard_map/all_to_all | solution.py:172
  16.0 2.1 collective-permute-start.1
  19.8 3.1 collective-permute-start.2
  27.9 69.3 %all_gather.3 = f32[3,16384]{1,0:T(4,128)S(1)} all-gather(f32[3,512]{1,0:T(4,128)S(1)} %copy-done.4), channel_id=1, replica_groups=mesh['bulk'=4,'grid'=8] {'bulk','grid'}, dimensions={1}, use_global_device_ids=true | all-gather | bytes 202752 | tf_op jit(solution)/shard_map/all_gather | solution.py:138
  97.4 300.2 %while.27 = (s32[]{:T(128)}, f32[3,3072]{1,0:T(4,128)S(1)}, f32[3,16384]{1,0:T(4,128)S(1)}, f32[3,3072]{1,0:T(4,128)S(1)}, f32[3,16384]{1,0:T(4,128)S(1)}, /*ind...) while((s32[]{:T(128)}, f32[3,3072]{1,0:T(4,128)S(1)}, ...), condition=%wide.region_1.2_spmd.clone, body=%wide.region_0.1_spmd.clone.sunk | while | flops 327174144 | bytes 303317 | solution.py:88
  97.6 37.3 %fusion.100 = f32[3,3072]{1,0:T(4,128)S(1)} fusion(f32[2048]{0:T(1024)S(1)} %bitcast.159, f32[3072]{0:T(1024)S(1)} %bitcast.152, f32[2048]{0:T(1024)S(1)} %bitcast.158, f32[3072]{0:T(1024)S(1)} %bitcast.153, f32[2048]{0:T(1024)S(1)} %bitcast.157, f32[3072]{0:T(1024)S(1)} %bitcast.151, f32[3,3072]{1,0:T(4,128)S(1)} %get-tuple-element.329, ...), kind=kOutput, calls=%fused_computation.44.clone.1 | convolution fusion | flops 327174144 | bytes 180229 | tf_op jit(solution)/shard_map/while/body/eval_jaxpr/ck,nk->cn/dot_general | solution.py:75
  135.1 37.3 %fusion.100 = f32[3,3072]{1,0:T(4,128)S(1)} fusion(f32[2048]{0:T(1024)S(1)} %bitcast.159, f32[3072]{0:T(1024)S(1)} %bitcast.152, f32[2048]{0:T(1024)S(1)} %bitcast.158, f32[3072]{0:T(1024)S(1)} %bitcast.153, f32[2048]{0:T(1024)S(1)} %bitcast.157, f32[3072]{0:T(1024)S(1)} %bitcast.151, f32[3,3072]{1,0:T(4,128)S(1)} %get-tuple-element.329, ...), kind=kOutput, calls=%fused_computation.44.clone.1 | convolution fusion | flops 327174144 | bytes 180229 | tf_op jit(solution)/shard_map/while/body/eval_jaxpr/ck,nk->cn/dot_general | solution.py:75
  172.6 37.3 %fusion.100 = f32[3,3072]{1,0:T(4,128)S(1)} fusion(f32[2048]{0:T(1024)S(1)} %bitcast.159, f32[3072]{0:T(1024)S(1)} %bitcast.152, f32[2048]{0:T(1024)S(1)} %bitcast.158, f32[3072]{0:T(1024)S(1)} %bitcast.153, f32[2048]{0:T(1024)S(1)} %bitcast.157, f32[3072]{0:T(1024)S(1)} %bitcast.151, f32[3,3072]{1,0:T(4,128)S(1)} %get-tuple-element.329, ...), kind=kOutput, calls=%fused_computation.44.clone.1 | convolution fusion | flops 327174144 | bytes 180229 | tf_op jit(solution)/shard_map/while/body/eval_jaxpr/ck,nk->cn/dot_general | solution.py:75
  210.1 37.3 %fusion.100 = f32[3,3072]{1,0:T(4,128)S(1)} fusion(f32[2048]{0:T(1024)S(1)} %bitcast.159, f32[3072]{0:T(1024)S(1)} %bitcast.152, f32[2048]{0:T(1024)S(1)} %bitcast.158, f32[3072]{0:T(1024)S(1)} %bitcast.153, f32[2048]{0:T(1024)S(1)} %bitcast.157, f32[3072]{0:T(1024)S(1)} %bitcast.151, f32[3,3072]{1,0:T(4,128)S(1)} %get-tuple-element.329, ...), kind=kOutput, calls=%fused_computation.44.clone.1 | convolution fusion | flops 327174144 | bytes 180229 | tf_op jit(solution)/shard_map/while/body/eval_jaxpr/ck,nk->cn/dot_general | solution.py:75
  247.6 37.3 %fusion.100 = f32[3,3072]{1,0:T(4,128)S(1)} fusion(f32[2048]{0:T(1024)S(1)} %bitcast.159, f32[3072]{0:T(1024)S(1)} %bitcast.152, f32[2048]{0:T(1024)S(1)} %bitcast.158, f32[3072]{0:T(1024)S(1)} %bitcast.153, f32[2048]{0:T(1024)S(1)} %bitcast.157, f32[3072]{0:T(1024)S(1)} %bitcast.151, f32[3,3072]{1,0:T(4,128)S(1)} %get-tuple-element.329, ...), kind=kOutput, calls=%fused_computation.44.clone.1 | convolution fusion | flops 327174144 | bytes 180229 | tf_op jit(solution)/shard_map/while/body/eval_jaxpr/ck,nk->cn/dot_general | solution.py:75
  285.1 37.3 %fusion.100 = f32[3,3072]{1,0:T(4,128)S(1)} fusion(f32[2048]{0:T(1024)S(1)} %bitcast.159, f32[3072]{0:T(1024)S(1)} %bitcast.152, f32[2048]{0:T(1024)S(1)} %bitcast.158, f32[3072]{0:T(1024)S(1)} %bitcast.153, f32[2048]{0:T(1024)S(1)} %bitcast.157, f32[3072]{0:T(1024)S(1)} %bitcast.151, f32[3,3072]{1,0:T(4,128)S(1)} %get-tuple-element.329, ...), kind=kOutput, calls=%fused_computation.44.clone.1 | convolution fusion | flops 327174144 | bytes 180229 | tf_op jit(solution)/shard_map/while/body/eval_jaxpr/ck,nk->cn/dot_general | solution.py:75
  322.6 37.3 %fusion.100 = f32[3,3072]{1,0:T(4,128)S(1)} fusion(f32[2048]{0:T(1024)S(1)} %bitcast.159, f32[3072]{0:T(1024)S(1)} %bitcast.152, f32[2048]{0:T(1024)S(1)} %bitcast.158, f32[3072]{0:T(1024)S(1)} %bitcast.153, f32[2048]{0:T(1024)S(1)} %bitcast.157, f32[3072]{0:T(1024)S(1)} %bitcast.151, f32[3,3072]{1,0:T(4,128)S(1)} %get-tuple-element.329, ...), kind=kOutput, calls=%fused_computation.44.clone.1 | convolution fusion | flops 327174144 | bytes 180229 | tf_op jit(solution)/shard_map/while/body/eval_jaxpr/ck,nk->cn/dot_general | solution.py:75
  360.1 37.3 %fusion.100 = f32[3,3072]{1,0:T(4,128)S(1)} fusion(f32[2048]{0:T(1024)S(1)} %bitcast.159, f32[3072]{0:T(1024)S(1)} %bitcast.152, f32[2048]{0:T(1024)S(1)} %bitcast.158, f32[3072]{0:T(1024)S(1)} %bitcast.153, f32[2048]{0:T(1024)S(1)} %bitcast.157, f32[3072]{0:T(1024)S(1)} %bitcast.151, f32[3,3072]{1,0:T(4,128)S(1)} %get-tuple-element.329, ...), kind=kOutput, calls=%fused_computation.44.clone.1 | convolution fusion | flops 327174144 | bytes 180229 | tf_op jit(solution)/shard_map/while/body/eval_jaxpr/ck,nk->cn/dot_general | solution.py:75
  403.9 3.6 all-to-all-start
  409.2 22.2 %all-to-all-done = f32[8,28,8,128]{3,2,1,0:T(8,128)S(1)} async-done(((f32[8,28,8,128]{3,2,1,0:T(8,128)}), f32[8,28,8,128]{3,2,1,0:T(8,128)S(1)}, u32[]{:S(2)}, u32[]{:S(2)}) %all-to-all-start) | async-done | bytes 917536 | tf_op jit(solution)/shard_map/all_to_all | solution.py:171
  431.5 56.5 %while.26 = (s32[]{:T(128)}, f32[8,28,5,128]{3,2,1,0:T(8,128)S(1)}, f32[8,28,8,128]{3,2,1,0:T(8,128)S(1)}, f32[8,28,3,128]{3,1,2,0:T(8,128)S(1)}, s32[]{:T(128)}) while((s32[]{:T(128)}, f32[8,28,5,128]{3,2,1,0:T(8,128)S(1)}, f32[8,28,8,128]{3,2,1,0:T(8,128)S(1)}, f32[8,28,3,128]{3,1,2,0:T(8,128)S(1)}, s32[]{:T(128)}) %tuple.90), condition=%wide.region_7.8_spmd, body=%wide.region_5.7_spmd.sunk | while | flops 37173248 | bytes 1017937 | solution.py:180
  431.6 2.4 fusion.95
  434.0 4.5 fusion.96
  438.6 2.4 fusion.95
  441.1 4.5 fusion.96
  445.7 2.4 fusion.95
  448.1 4.5 fusion.96
  452.8 2.4 fusion.95
  455.2 4.5 fusion.96
  459.8 2.4 fusion.95
  462.3 4.5 fusion.96
  466.9 2.4 fusion.95
  469.3 4.5 fusion.96
  474.0 2.4 fusion.95
  476.4 4.5 fusion.96
  481.0 2.4 fusion.95
  483.5 4.5 fusion.96
  (134 shorter events, 25.1 us)
Async XLA Ops:
  0.6 27.2 %copy-start.1 = (f32[1,3,1,24,128]{4,3,2,1,0:T(8,128)S(1)}, f32[1,3,1,24,128]{4,3,2,1,0:T(8,128)}, u32[]{:S(2)}) copy-start(f32[1,3,1,24,128]{4,3,2,1,0:T(8,128)} %param.11) | copy-start | bytes 110596
  0.6 27.3 %copy-start.4 = (f32[3,512]{1,0:T(4,128)S(1)}, f32[3,512]{1,0:T(4,128)}, u32[]{:S(2)}) copy-start(f32[3,512]{1,0:T(4,128)} %param.13) | copy-start | bytes 18436
  4.1 399.9 %all-to-all-start.1 = ((f32[8,1,28]{2,1,0:T(1,128)}), f32[8,1,28]{2,1,0:T(1,128)S(1)}, u32[]{:S(2)}, u32[]{:S(2)}) async-start(f32[8,1,28]{2,1,0:T(1,128)} %convolution_bitcast_fusion.1), calls=%async_computation.1 | async-start | bytes 8192 | tf_op jit(solution)/shard_map/all_to_all | solution.py:172
  11.4 3.9 collective-permute-start
  16.0 3.8 collective-permute-start.1
  19.8 5.0 %collective-permute-start.2 = (f32[4,3,512]{2,1,0:T(4,128)S(1)}, f32[4,3,512]{2,1,0:T(4,128)S(1)}, u32[]{:S(2)}, u32[]{:S(2)}) collective-permute-start(f32[4,3,512]{2,1,0:T(4,128)S(1)} %bitcast.160), channel_id=1, source_target_pairs={{0,4},{1,5},{2,6},{3,7},{4,0},{5,1},{6,2},{7,3},{8,12},{9,13},{10,... | collective-permute-start | bytes 73736 | tf_op jit(solution)/shard_map/ppermute | solution.py:24
  24.9 1.3 collective-permute-start.3
  26.3 70.9 %collective-permute-start.4 = (f32[16,3,512]{2,0,1:T(8,128)S(1)}, f32[16,3,512]{2,0,1:T(8,128)S(1)}, u32[]{:S(2)}, u32[]{:S(2)}) collective-permute-start(f32[16,3,512]{2,0,1:T(8,128)S(1)} %bitcast.148), channel_id=1, source_target_pairs={{0,16},{1,17},{2,18},{3,19},{4,20},{5,21},{6,22},{7,23},{8,24},{9,... | collective-permute-start | bytes 294920 | tf_op jit(solution)/shard_map/ppermute | solution.py:24
  397.6 3.6 copy-start.2
  397.6 3.6 copy-start.5
  397.7 11.1 %copy-start = (f32[1,3,1,24,128]{4,3,1,2,0:T(8,128)}, f32[1,3,1,24,128]{4,3,1,2,0:T(8,128)S(1)}, u32[]{:S(2)}) copy-start(f32[1,3,1,24,128]{4,3,1,2,0:T(8,128)S(1)} %bitcast_add_fusion) | copy-start | bytes 110596
  397.8 3.4 collective-permute-start.6
  397.8 3.4 collective-permute-start.5
  401.2 1.2 copy-start.3
  403.9 27.5 %all-to-all-start = ((f32[8,28,8,128]{3,2,1,0:T(8,128)}), f32[8,28,8,128]{3,2,1,0:T(8,128)S(1)}, u32[]{:S(2)}, u32[]{:S(2)}) async-start(f32[8,28,8,128]{3,2,1,0:T(8,128)} %bitcast.36), calls=%async_computation | async-start | bytes 1835008 | tf_op jit(solution)/shard_map/all_to_all | solution.py:171
